TPU v7x, 512 devices: a whole 4x8x8 slice. The times are simulated.
512 devices in a mesh: row: 32 (over y, x), col: 16 (over z, core).
Axes of the slice: x: 4, y: 8, z: 8, core: 2. Of those that a mesh axis runs over, the one named last changes fastest.
Arguments:
- right_side: float32 [64, 16384], P(None, ('row', 'col')), may hold values from -6 to 6
- regular: float32 [16384], P(('row', 'col')), may hold values from 1 to 2
- curvature: bfloat16 [32, 32, 16, 128, 128], P('row', None, 'col'), as said below
- block_rows: int32 [32, 32, 16], P('row', None, 'col'), may hold values from 0 to 3, as said below
- block_cols: int32 [32, 32, 16], P('row', None, 'col'), may hold values from 0 to 3
- block_counts: int32 [32, 32, 16], P('row', None, 'col'), may hold values from 0 to 1, as said below
Outputs:
- solution: float32 [64, 16384], P(None, ('row', 'col'))
- residual: float32 [64, 16384], P(None, ('row', 'col'))
Inputs may be any that keep to these rules, and one draw needn't show every extreme that they name: `block_rows`: the curvature is symmetric: a live term of owner r from source s with block row a and block column b is matched, in the same slot of owner s from source r, by block row b, block column a and the transposed block. `block_counts`: counts for the first index of col are always 1. A with this curvature and regular is symmetric positive definite.
All inputs are finite; a program needn't handle non-finite values.
Results may differ from a plain program's by a relative error of at most 0.0041.
Values may be sent and summed in bfloat16 or wider, within the bound.
No kernel may reach another device: no remote copies, remote signals or barrier semaphores. Data moves between devices by JAX's collectives and lax.ppermute only.
A program may use at most 64 MiB of HBM per device.

v0:
```python
import jax
import jax.numpy as jnp
from jax import lax
from jax.sharding import Mesh
from jax.sharding import PartitionSpec as P

M_DEV = 1
ITERS = 3
COL = ("col_0", "col_1")
ROW_COL = ("row_0", "row_1", "col_0", "col_1")
ROW = ("row_0", "row_1")


def one_axis_at_a_time(shard, axes):
    for axis in axes:
        shard = lax.psum(shard, axis)
    return shard


def gather_axes(shard, axes, dim):
    for axis in reversed(axes):
        shard = lax.all_gather(shard, axis, axis=dim, tiled=True)
    return shard


def in_blocks(shard, dim, peers):
    shape = shard.shape
    blocks = shard.reshape(*shape[:dim], peers, shape[dim] // peers, *shape[dim + 1 :])
    return jnp.moveaxis(blocks, dim, 0)


def sum_at_owner(shard, axis, dim):
    peers = lax.axis_size(axis)
    blocks = lax.all_to_all(in_blocks(shard, dim, peers), axis, 0, 0, tiled=True)
    return jnp.sum(blocks, axis=0)


def chol_solve(matrix, rhs_mat):
    factor = jnp.linalg.cholesky(matrix)
    return jax.scipy.linalg.cho_solve((factor, True), rhs_mat)


def local_gram(left, right):
    return jnp.dot(left, right.T, precision=lax.Precision.HIGHEST)


def live_table(counts_local):
    per_slot = jnp.repeat(counts_local, M_DEV, axis=1)
    slot_rank = jnp.arange(per_slot.shape[1], dtype=jnp.int32) % M_DEV
    return slot_rank[None, :] < per_slot


def apply_terms(dir_piece, curv_local, rows_local, cols_local, live_local, blocks_dev):
    samples = dir_piece.shape[0]
    sources = dir_piece.shape[1]
    block_len = curv_local.shape[-1]
    slot_cap = curv_local.shape[1]
    flat_dirs = dir_piece.reshape(samples, sources * blocks_dev, block_len)
    positions = (jnp.arange(sources, dtype=jnp.int32)[:, None] * blocks_dev + cols_local).reshape(
        -1
    )
    chosen = jnp.take(flat_dirs, positions, axis=1).reshape(samples, sources, slot_cap, block_len)
    products = jnp.einsum("xsmq,smpq->xsmp", chosen, curv_local, preferred_element_type=jnp.float32)
    block_ids = jnp.arange(blocks_dev, dtype=jnp.int32)
    row_table = (
        (rows_local[:, :, None] == block_ids[None, None, :]) & live_local[:, :, None]
    ).astype(jnp.float32)
    return jnp.einsum("xsmp,smb->xbp", products, row_table, precision=lax.Precision.HIGHEST)


def body(right_side, regular, curvature, block_rows, block_cols, block_counts):
    samples = right_side.shape[0]
    pix_here = right_side.shape[1]
    block_len = curvature.shape[-1]
    blocks_dev = pix_here * lax.axis_size(COL) // block_len
    curv_local = curvature[0]
    rows_local = block_rows[0]
    cols_local = block_cols[0]
    live_local = live_table(block_counts[0])
    solution = jnp.zeros_like(right_side)
    residual = right_side
    direction = right_side
    res_gram = one_axis_at_a_time(local_gram(residual, residual), ROW_COL)
    for iteration in range(ITERS):
        dir_bf = direction.astype(jnp.bfloat16)
        own_rows = lax.all_gather(dir_bf, COL, axis=1, tiled=True)
        partials = apply_terms(
            gather_axes(own_rows[:, None, :], ROW, 1),
            curv_local,
            rows_local,
            cols_local,
            live_local,
            blocks_dev,
        )
        coupled = sum_at_owner(partials.reshape(samples, blocks_dev * block_len), COL, 1)
        image = regular[None, :] * direction + coupled
        curv_gram, cross_gram, image_gram = (
            one_axis_at_a_time(local_gram(direction, image), ROW_COL),
            one_axis_at_a_time(local_gram(residual, image), ROW_COL),
            one_axis_at_a_time(local_gram(image, image), ROW_COL),
        )
        curv_gram = 0.5 * (curv_gram + curv_gram.T)
        alpha_mat = chol_solve(curv_gram, res_gram)
        solution = solution + jnp.dot(alpha_mat.T, direction, precision=lax.Precision.HIGHEST)
        residual = residual - jnp.dot(alpha_mat.T, image, precision=lax.Precision.HIGHEST)
        cross_term = jnp.dot(cross_gram, alpha_mat, precision=lax.Precision.HIGHEST)
        quad_term = jnp.dot(
            alpha_mat.T,
            jnp.dot(image_gram, alpha_mat, precision=lax.Precision.HIGHEST),
            precision=lax.Precision.HIGHEST,
        )
        new_gram = res_gram - cross_term - cross_term.T + quad_term
        new_gram = 0.5 * (new_gram + new_gram.T)
        if iteration + 1 < ITERS:
            beta_mat = chol_solve(res_gram, new_gram)
            direction = residual + jnp.dot(beta_mat.T, direction, precision=lax.Precision.HIGHEST)
            res_gram = new_gram
    return (solution, residual)


def solution(mesh):
    finer = Mesh(mesh.devices.reshape(8, 4, 8, 2), ("row_0", "row_1", "col_0", "col_1"))
    placed = (
        P(None, ROW_COL),
        P(ROW_COL),
        P(ROW, None, COL, None, None),
        P(ROW, None, COL),
        P(ROW, None, COL),
        P(ROW, None, COL),
    )
    return jax.shard_map(
        body,
        mesh=finer,
        in_specs=placed,
        out_specs=(P(None, ROW_COL), P(None, ROW_COL)),
        check_vma=False,
    )
```

profile of v0, /device:TPU:1, one launch (start us, length us, event | category | flops | bytes accessed | tf_op | source)
XLA Modules:
  0.0 618.6 jit_solution(11180150527277156011)
XLA Ops:
  8.0 24.8 %all_gather.27 = bf16[64,512]{0,1:T(8,128)(2,1)S(1)} all-gather(bf16[64,32]{0,1:T(8,128)(2,1)S(1)} %convert_element_type.12), channel_id=1, replica_groups=mesh['row_0'=8,'row_1'=4,'col_0'=8,'col_1'=2] {'col_0','col_1'}, dimensions={1}, use_global_device_ids=true | all-gather | bytes 69632 | tf_op jit(solution)/shard_map/all_gather | solution.py:86
  32.8 11.0 %all-gather = bf16[64,2048]{0,1:T(8,128)(2,1)S(1)} all-gather(bf16[64,512]{0,1:T(8,128)(2,1)S(1)} %all_gather.27), channel_id=2, replica_groups=mesh['row_0'=8,'row_1'=4,'col_0'=8,'col_1'=2] {'row_1'}, dimensions={1}, use_global_device_ids=true | all-gather | bytes 327680 | tf_op jit(solution)/shard_map/all_gather | solution.py:22
  46.1 36.7 %all-gather.7.cloned.1.call-done = bf16[64,32,512]{2,0,1:T(8,128)(2,1)} async-done(((bf16[64,4,512]{2,0,1:T(8,128)(2,1)}), bf16[64,32,512]{2,0,1:T(8,128)(2,1)}) %all-gather.7.cloned.1.call-update) | async-done | bytes 2097168 | tf_op jit(solution)/shard_map/all_gather | solution.py:22
  82.9 2.8 copy.113
  85.6 2.6 reshape.187
  88.2 2.9 copy.114
  92.6 1.9 convolution_bitcast_fusion.2
  96.5 12.2 %all-to-all-start = ((f32[16,1,2048]{2,1,0:T(1,128)}), f32[16,1,2048]{2,1,0:T(1,128)S(1)}, u32[]{:S(2)}, u32[]{:S(2)}) async-start(f32[16,1,2048]{2,1,0:T(1,128)} %reshape.231), calls=%async_computation | async-start | bytes 262144 | tf_op jit(solution)/shard_map/all_to_all | solution.py:34
  109.0 8.6 %all-to-all-done = f32[16,1,2048]{2,1,0:T(1,128)S(1)} async-done(((f32[16,1,2048]{2,1,0:T(1,128)}), f32[16,1,2048]{2,1,0:T(1,128)S(1)}, u32[]{:S(2)}, u32[]{:S(2)}) %all-to-all-start) | async-done | bytes 131104 | tf_op jit(solution)/shard_map/all_to_all | solution.py:34
  119.8 22.9 %all-reduce.3 = (f32[64,64]{0,1:T(8,128)S(1)}, f32[64,64]{1,0:T(8,128)S(1)}, f32[64,64]{1,0:T(8,128)S(1)}) all-reduce(f32[64,64]{0,1:T(8,128)S(1)} %fusion.74, f32[64,64]{1,0:T(8,128)S(1)} %convolution_bitcast_fusion.6, f32[64,64]{1,0:T(8,128)S(1)} %fusion.54), channel_id=1, replica_groups=mesh['row_0'=8,'row_1'=4,'col_0'=8,'col_1'=2] {'row_0'}, use_global_device_ids=true, to_apply=%region_7.10 | all-reduce | flops 12288 | bytes 98304 | tf_op jit(solution)/shard_map/psum | solution.py:16
  142.7 14.2 %all-reduce.5 = (f32[64,64]{0,1:T(8,128)S(1)}, f32[64,64]{1,0:T(8,128)S(1)}, f32[64,64]{1,0:T(8,128)S(1)}) all-reduce(f32[64,64]{0,1:T(8,128)S(1)} %get-tuple-element.14, f32[64,64]{1,0:T(8,128)S(1)} %get-tuple-element.15, f32[64,64]{1,0:T(8,128)S(1)} %get-tuple-element.16), channel_id=1, replica_groups=mesh['row_0'=8,'row_1'=4,'col_0'=8,'col_1'=2] {'row_1'}, use_global_device_ids=true, to_apply=%region_8.11 | all-reduce | flops 12288 | bytes 98304 | tf_op jit(solution)/shard_map/psum | solution.py:16
  156.9 21.7 %all-reduce.1 = (f32[64,64]{0,1:T(8,128)S(1)}, f32[64,64]{1,0:T(8,128)S(1)}, f32[64,64]{1,0:T(8,128)S(1)}) all-reduce(f32[64,64]{0,1:T(8,128)S(1)} %get-tuple-element.20, f32[64,64]{1,0:T(8,128)S(1)} %get-tuple-element.21, f32[64,64]{1,0:T(8,128)S(1)} %get-tuple-element.22), channel_id=1, replica_groups=mesh['row_0'=8,'row_1'=4,'col_0'=8,'col_1'=2] {'col_0'}, use_global_device_ids=true, to_apply=%region_9.12 | all-reduce | flops 12288 | bytes 98304 | tf_op jit(solution)/shard_map/psum | solution.py:16
  178.6 21.3 %all-reduce.7 = (f32[64,64]{0,1:T(8,128)S(1)}, f32[64,64]{1,0:T(8,128)S(1)}, f32[64,64]{1,0:T(8,128)S(1)}) all-reduce(f32[64,64]{0,1:T(8,128)S(1)} %get-tuple-element.8, f32[64,64]{1,0:T(8,128)S(1)} %get-tuple-element.9, f32[64,64]{1,0:T(8,128)S(1)} %get-tuple-element.10), channel_id=1, replica_groups=mesh['row_0'=8,'row_1'=4,'col_0'=8,'col_1'=2] {'col_1'}, use_global_device_ids=true, to_apply=%region_10.13 | all-reduce | flops 12288 | bytes 98304 | tf_op jit(solution)/shard_map/psum | solution.py:16
  200.1 5.8 cholesky.89
  207.3 4.9 custom-call.11
  213.7 5.8 cholesky.100
  220.9 4.9 custom-call.12
  226.3 15.8 %all_gather.30 = bf16[64,512]{0,1:T(8,128)(2,1)S(1)} all-gather(bf16[64,32]{0,1:T(8,128)(2,1)S(1)} %get-tuple-element.31), channel_id=1, replica_groups=mesh['row_0'=8,'row_1'=4,'col_0'=8,'col_1'=2] {'col_0','col_1'}, dimensions={1}, use_global_device_ids=true | all-gather | bytes 69632 | tf_op jit(solution)/shard_map/all_gather | solution.py:86
  242.2 10.3 %all-gather.1 = bf16[64,2048]{0,1:T(8,128)(2,1)S(1)} all-gather(bf16[64,512]{0,1:T(8,128)(2,1)S(1)} %all_gather.30), channel_id=3, replica_groups=mesh['row_0'=8,'row_1'=4,'col_0'=8,'col_1'=2] {'row_1'}, dimensions={1}, use_global_device_ids=true | all-gather | bytes 327680 | tf_op jit(solution)/shard_map/all_gather | solution.py:22
  253.6 5.9 cholesky.122
  259.4 30.4 %all-gather.9.cloned.1.call-done = bf16[64,32,512]{2,0,1:T(8,128)(2,1)} async-done(((bf16[64,4,512]{2,0,1:T(8,128)(2,1)}), bf16[64,32,512]{2,0,1:T(8,128)(2,1)}) %all-gather.9.cloned.1.call-update) | async-done | bytes 2097168 | tf_op jit(solution)/shard_map/all_gather | solution.py:22
  289.9 2.8 copy.127
  292.6 2.6 reshape.190
  295.2 2.9 copy.128
  303.5 12.2 %all-to-all-start.1 = ((f32[16,1,2048]{2,1,0:T(1,128)}), f32[16,1,2048]{2,1,0:T(1,128)S(1)}, u32[]{:S(2)}, u32[]{:S(2)}) async-start(f32[16,1,2048]{2,1,0:T(1,128)} %reshape.233), calls=%async_computation.1 | async-start | bytes 262144 | tf_op jit(solution)/shard_map/all_to_all | solution.py:34
  317.2 4.9 custom-call.14
  322.1 2.4 all-to-all-done.1
  326.5 22.9 %all-reduce.2 = (f32[64,64]{1,0:T(8,128)S(1)}, f32[64,64]{1,0:T(8,128)S(1)}, f32[64,64]{1,0:T(8,128)S(1)}) all-reduce(f32[64,64]{1,0:T(8,128)S(1)} %fusion.78, f32[64,64]{1,0:T(8,128)S(1)} %fusion.81, f32[64,64]{1,0:T(8,128)S(1)} %fusion.79), channel_id=1, replica_groups=mesh['row_0'=8,'row_1'=4,'col_0'=8,'col_1'=2] {'row_0'}, use_global_device_ids=true, to_apply=%region_16.20 | all-reduce | flops 12288 | bytes 98304 | tf_op jit(solution)/shard_map/psum | solution.py:16
  349.4 14.2 %all-reduce.4 = (f32[64,64]{1,0:T(8,128)S(1)}, f32[64,64]{1,0:T(8,128)S(1)}, f32[64,64]{1,0:T(8,128)S(1)}) all-reduce(f32[64,64]{1,0:T(8,128)S(1)} %get-tuple-element.11, f32[64,64]{1,0:T(8,128)S(1)} %get-tuple-element.12, f32[64,64]{1,0:T(8,128)S(1)} %get-tuple-element.13), channel_id=1, replica_groups=mesh['row_0'=8,'row_1'=4,'col_0'=8,'col_1'=2] {'row_1'}, use_global_device_ids=true, to_apply=%region_17.21 | all-reduce | flops 12288 | bytes 98304 | tf_op jit(solution)/shard_map/psum | solution.py:16
  363.6 21.6 %all-reduce = (f32[64,64]{1,0:T(8,128)S(1)}, f32[64,64]{1,0:T(8,128)S(1)}, f32[64,64]{1,0:T(8,128)S(1)}) all-reduce(f32[64,64]{1,0:T(8,128)S(1)} %get-tuple-element.17, f32[64,64]{1,0:T(8,128)S(1)} %get-tuple-element.18, f32[64,64]{1,0:T(8,128)S(1)} %get-tuple-element.19), channel_id=1, replica_groups=mesh['row_0'=8,'row_1'=4,'col_0'=8,'col_1'=2] {'col_0'}, use_global_device_ids=true, to_apply=%region_18.22 | all-reduce | flops 12288 | bytes 98304 | tf_op jit(solution)/shard_map/psum | solution.py:16
  385.2 21.5 %all-reduce.6 = (f32[64,64]{1,0:T(8,128)S(1)}, f32[64,64]{1,0:T(8,128)S(1)}, f32[64,64]{1,0:T(8,128)S(1)}) all-reduce(f32[64,64]{1,0:T(8,128)S(1)} %get-tuple-element.4, f32[64,64]{1,0:T(8,128)S(1)} %get-tuple-element.6, f32[64,64]{1,0:T(8,128)S(1)} %get-tuple-element.7), channel_id=1, replica_groups=mesh['row_0'=8,'row_1'=4,'col_0'=8,'col_1'=2] {'col_1'}, use_global_device_ids=true, to_apply=%region_19.23 | all-reduce | flops 12288 | bytes 98304 | tf_op jit(solution)/shard_map/psum | solution.py:16
  406.9 5.8 cholesky.111
  414.1 4.9 custom-call.13
  420.9 15.6 %all_gather.33 = bf16[64,512]{0,1:T(8,128)(2,1)S(1)} all-gather(bf16[64,32]{0,1:T(8,128)(2,1)S(1)} %get-tuple-element.33), channel_id=1, replica_groups=mesh['row_0'=8,'row_1'=4,'col_0'=8,'col_1'=2] {'col_0','col_1'}, dimensions={1}, use_global_device_ids=true | all-gather | bytes 69632 | tf_op jit(solution)/shard_map/all_gather | solution.py:86
  436.4 10.3 %all-gather.2 = bf16[64,2048]{0,1:T(8,128)(2,1)S(1)} all-gather(bf16[64,512]{0,1:T(8,128)(2,1)S(1)} %all_gather.33), channel_id=4, replica_groups=mesh['row_0'=8,'row_1'=4,'col_0'=8,'col_1'=2] {'row_1'}, dimensions={1}, use_global_device_ids=true | all-gather | bytes 327680 | tf_op jit(solution)/shard_map/all_gather | solution.py:22
  447.6 37.4 %all-gather.11.cloned.1.call-done = bf16[64,32,512]{2,0,1:T(8,128)(2,1)} async-done(((bf16[64,4,512]{2,0,1:T(8,128)(2,1)}), bf16[64,32,512]{2,0,1:T(8,128)(2,1)}) %all-gather.11.cloned.1.call-update) | async-done | bytes 2097168 | tf_op jit(solution)/shard_map/all_gather | solution.py:22
  485.1 2.8 copy.138
  487.8 2.6 reshape.192
  490.4 2.9 copy.139
  494.8 1.9 convolution_bitcast_fusion
  498.7 12.2 %all-to-all-start.2 = ((f32[16,1,2048]{2,1,0:T(1,128)}), f32[16,1,2048]{2,1,0:T(1,128)S(1)}, u32[]{:S(2)}, u32[]{:S(2)}) async-start(f32[16,1,2048]{2,1,0:T(1,128)} %reshape.235), calls=%async_computation.2 | async-start | bytes 262144 | tf_op jit(solution)/shard_map/all_to_all | solution.py:34
  511.2 8.6 %all-to-all-done.2 = f32[16,1,2048]{2,1,0:T(1,128)S(1)} async-done(((f32[16,1,2048]{2,1,0:T(1,128)}), f32[16,1,2048]{2,1,0:T(1,128)S(1)}, u32[]{:S(2)}, u32[]{:S(2)}) %all-to-all-start.2) | async-done | bytes 131104 | tf_op jit(solution)/shard_map/all_to_all | solution.py:34
  521.1 22.1 %psum.232 = f32[64,64]{1,0:T(8,128)S(1)} all-reduce(f32[64,64]{1,0:T(8,128)S(1)} %fusion.53), channel_id=1, replica_groups=mesh['row_0'=8,'row_1'=4,'col_0'=8,'col_1'=2] {'row_0'}, use_global_device_ids=true, to_apply=%region_29.33 | all-reduce | flops 4096 | bytes 32768 | tf_op jit(solution)/shard_map/psum | solution.py:16
  543.2 13.2 %psum.233 = f32[64,64]{1,0:T(8,128)S(1)} all-reduce(f32[64,64]{1,0:T(8,128)S(1)} %psum.232), channel_id=1, replica_groups=mesh['row_0'=8,'row_1'=4,'col_0'=8,'col_1'=2] {'row_1'}, use_global_device_ids=true, to_apply=%region_30.34 | all-reduce | flops 4096 | bytes 32768 | tf_op jit(solution)/shard_map/psum | solution.py:16
  556.4 20.4 %psum.234 = f32[64,64]{1,0:T(8,128)S(1)} all-reduce(f32[64,64]{1,0:T(8,128)S(1)} %psum.233), channel_id=1, replica_groups=mesh['row_0'=8,'row_1'=4,'col_0'=8,'col_1'=2] {'col_0'}, use_global_device_ids=true, to_apply=%region_31.35 | all-reduce | flops 4096 | bytes 32768 | tf_op jit(solution)/shard_map/psum | solution.py:16
  576.8 21.0 %psum.235 = f32[64,64]{1,0:T(8,128)S(1)} all-reduce(f32[64,64]{1,0:T(8,128)S(1)} %psum.234), channel_id=1, replica_groups=mesh['row_0'=8,'row_1'=4,'col_0'=8,'col_1'=2] {'col_1'}, use_global_device_ids=true, to_apply=%region_32.36 | all-reduce | flops 4096 | bytes 32768 | tf_op jit(solution)/shard_map/psum | solution.py:16
  598.0 5.8 cholesky.133
  605.2 4.9 custom-call.15
  (113 shorter events, 36.3 us)
Async XLA Ops:
  7.2 85.4 %copy-start = (bf16[1,32,1,128,128]{4,3,2,1,0:T(8,128)(2,1)S(1)}, bf16[1,32,1,128,128]{4,3,2,1,0:T(8,128)(2,1)}, u32[]{:S(2)}) copy-start(bf16[1,32,1,128,128]{4,3,2,1,0:T(8,128)(2,1)} %param.13) | copy-start | bytes 3145732
  7.2 75.7 %all-gather.7.cloned.1.call-start = ((), (), s32[]{:S(2)}) async-start(), calls=%async_computation.3 | async-start | bytes 2359296 | tf_op jit(solution)/shard_map/all_gather | solution.py:22
  91.2 3.3 copy-start.3
  92.6 16.2 %copy-start.1 = (f32[64,32]{0,1:T(8,128)S(1)}, f32[64,32]{0,1:T(8,128)}, u32[]{:S(2)}) copy-start(f32[64,32]{0,1:T(8,128)} %param.11) | copy-start | bytes 24580
  94.5 24.7 %copy-start.2 = (f32[32]{0:T(128)S(1)}, f32[32]{0:T(128)}, u32[]{:S(2)}) copy-start(f32[32]{0:T(128)} %param.12) | copy-start | bytes 388
  96.5 21.1 %all-to-all-start = ((f32[16,1,2048]{2,1,0:T(1,128)}), f32[16,1,2048]{2,1,0:T(1,128)S(1)}, u32[]{:S(2)}, u32[]{:S(2)}) async-start(f32[16,1,2048]{2,1,0:T(1,128)} %reshape.231), calls=%async_computation | async-start | bytes 262144 | tf_op jit(solution)/shard_map/all_to_all | solution.py:34
  108.7 181.2 %all-gather.9.cloned.1.call-start = ((), (), s32[]{:S(2)}) async-start(), calls=%async_computation.4 | async-start | bytes 2359296 | tf_op jit(solution)/shard_map/all_gather | solution.py:22
  303.5 21.1 %all-to-all-start.1 = ((f32[16,1,2048]{2,1,0:T(1,128)}), f32[16,1,2048]{2,1,0:T(1,128)S(1)}, u32[]{:S(2)}, u32[]{:S(2)}) async-start(f32[16,1,2048]{2,1,0:T(1,128)} %reshape.233), calls=%async_computation.1 | async-start | bytes 262144 | tf_op jit(solution)/shard_map/all_to_all | solution.py:34
  315.7 169.4 %all-gather.11.cloned.1.call-start = ((), (), s32[]{:S(2)}) async-start(), calls=%async_computation.5 | async-start | bytes 2359296 | tf_op jit(solution)/shard_map/all_gather | solution.py:22
  498.7 21.1 %all-to-all-start.2 = ((f32[16,1,2048]{2,1,0:T(1,128)}), f32[16,1,2048]{2,1,0:T(1,128)S(1)}, u32[]{:S(2)}, u32[]{:S(2)}) async-start(f32[16,1,2048]{2,1,0:T(1,128)} %reshape.235), calls=%async_computation.2 | async-start | bytes 262144 | tf_op jit(solution)/shard_map/all_to_all | solution.py:34
Sparse Core Ops, SparseCore 0:
  44.9 37.8 all-gather.6
  253.5 36.3 all-gather.8
  447.8 37.2 all-gather.10
where the time goes:
time: 620 us; the launch traced here: 619 us
  blocking collectives  325 us (52%)
  waiting for transfers between devices  124 us (20%)
  other arithmetic  65.6 us (11%)
  starting transfers between devices  37 us (6%)
  local copies, waits for them, and re-layouts  36.5 us (6%)
  matrix products  16.2 us (3%)
  between operations  14.4 us (2%)
    psum x12, blocking collectives, one_axis_at_a_time(): shard = lax.psum(shard, axis)  237 us
    all_gather x3, waiting for transfers between devices, gather_axes(): shard = lax.all_gather(shard, axis, axis=dim, tiled=True)  105 us
    all_gather x3, blocking collectives, body(): own_rows = lax.all_gather(dir_bf, COL, axis=1, tiled=True)  56.2 us
    all_to_all x3, starting transfers between devices, sum_at_owner(): lax.all_to_all(in_blocks(shard, dim, peers), axis, 0, 0, tiled=True)  36.7 us
    another operation x15, other arithmetic, chol_solve(): factor = jnp.linalg.cholesky(matrix)  32.6 us
    all_gather x3, blocking collectives, gather_axes(): shard = lax.all_gather(shard, axis, axis=dim, tiled=True)  31.5 us
    another operation x10, other arithmetic, chol_solve(): return jax.scipy.linalg.cho_solve((factor, True), rhs_mat)  27.7 us
    all_to_all x3, waiting for transfers between devices, sum_at_owner(): lax.all_to_all(in_blocks(shard, dim, peers), axis, 0, 0, tiled=True)  19.6 us
  transfers between devices with their start and end apart: 6, of which 6 were waited for; matrix products, arithmetic and copies ran while one was open for 2% of the time, Pallas kernels for 0%

commit v1 on v0

--- a/solution.py
+++ b/solution.py
@@ -83,7 +83,9 @@
     res_gram = one_axis_at_a_time(local_gram(residual, residual), ROW_COL)
     for iteration in range(ITERS):
         dir_bf = direction.astype(jnp.bfloat16)
-        own_rows = lax.all_gather(dir_bf, COL, axis=1, tiled=True)
+        own_rows = jnp.concatenate(
+            lax.all_to_all(jnp.stack([dir_bf] * lax.axis_size(COL)), COL, 0, 0), axis=1
+        )
         partials = apply_terms(
             gather_axes(own_rows[:, None, :], ROW, 1),
             curv_local,

time: 620 us -> 601 us (0.969)
  blocking collectives: 325 us -> 312 us
    all_gather x3 -> x0, blocking collectives: 56.2 us -> none  [body(): own_rows = lax.all_gather(dir_bf, COL, axis=1, tiled=True)]
    all_to_all x0 -> x3, blocking collectives: none -> 44.2 us  [body(): lax.all_to_all(jnp.stack([dir_bf] * lax.axis_size(COL)), COL, 0, 0)]
where the time goes in v1:
time: 601 us; the launch traced here: 600 us
  blocking collectives  312 us (52%)
  waiting for transfers between devices  120 us (20%)
  other arithmetic  65.6 us (11%)
  starting transfers between devices  36.9 us (6%)
  local copies, waits for them, and re-layouts  34.9 us (6%)
  matrix products  16.2 us (3%)
  between operations  14.5 us (2%)
    psum x12, blocking collectives, one_axis_at_a_time(): shard = lax.psum(shard, axis)  237 us
    all_gather x3, waiting for transfers between devices, gather_axes(): shard = lax.all_gather(shard, axis, axis=dim, tiled=True)  100 us
    all_to_all x3, blocking collectives, body(): lax.all_to_all(jnp.stack([dir_bf] * lax.axis_size(COL)), COL, 0, 0)  44.2 us
    all_to_all x3, starting transfers between devices, sum_at_owner(): lax.all_to_all(in_blocks(shard, dim, peers), axis, 0, 0, tiled=True)  36.6 us
    another operation x15, other arithmetic, chol_solve(): factor = jnp.linalg.cholesky(matrix)  32.6 us
    all_gather x3, blocking collectives, gather_axes(): shard = lax.all_gather(shard, axis, axis=dim, tiled=True)  30.7 us
    another operation x10, other arithmetic, chol_solve(): return jax.scipy.linalg.cho_solve((factor, True), rhs_mat)  27.7 us
    all_to_all x3, waiting for transfers between devices, sum_at_owner(): lax.all_to_all(in_blocks(shard, dim, peers), axis, 0, 0, tiled=True)  19.6 us
  transfers between devices with their start and end apart: 6, of which 6 were waited for; matrix products, arithmetic and copies ran while one was open for 2% of the time, Pallas kernels for 0%

profile of v1, /device:TPU:1, one launch (start us, length us, event | category | flops | bytes accessed | tf_op | source)
XLA Modules:
  0.0 600.0 jit_solution(7826365500098160287)
XLA Ops:
  8.2 19.4 %all_to_all.30 = bf16[16,2,1024]{2,1,0:T(2,128)(2,1)S(1)} all-to-all(bf16[16,2,1024]{2,1,0:T(2,128)(2,1)S(1)} %reshape.246), channel_id=1, replica_groups=mesh['row_0'=8,'row_1'=4,'col_0'=8,'col_1'=2] {'col_0','col_1'}, dimensions={0} | all-to-all | bytes 131072 | tf_op jit(solution)/shard_map/all_to_all | solution.py:87
  27.8 10.5 %all_gather.18 = bf16[64,4,512]{2,0,1:T(8,128)(2,1)} all-gather(bf16[64,1,512]{2,0,1:T(8,128)(2,1)S(1)} %copy.83), channel_id=1, replica_groups=mesh['row_0'=8,'row_1'=4,'col_0'=8,'col_1'=2] {'row_1'}, dimensions={1}, use_global_device_ids=true | all-gather | bytes 327680 | tf_op jit(solution)/shard_map/all_gather | solution.py:22
  39.6 36.6 %all-gather.4.cloned.1.call-done = bf16[64,32,512]{2,0,1:T(8,128)(2,1)} async-done(((bf16[64,4,512]{2,0,1:T(8,128)(2,1)}), bf16[64,32,512]{2,0,1:T(8,128)(2,1)}) %all-gather.4.cloned.1.call-update) | async-done | bytes 2097168 | tf_op jit(solution)/shard_map/all_gather | solution.py:22
  76.3 2.8 copy.84
  79.1 2.6 reshape.203
  81.6 2.9 copy.85
  86.0 1.9 convolution_bitcast_fusion.2
  89.9 12.2 %all-to-all-start.1 = ((f32[16,1,2048]{2,1,0:T(1,128)}), f32[16,1,2048]{2,1,0:T(1,128)S(1)}, u32[]{:S(2)}, u32[]{:S(2)}) async-start(f32[16,1,2048]{2,1,0:T(1,128)} %reshape.248), calls=%async_computation.1 | async-start | bytes 262144 | tf_op jit(solution)/shard_map/all_to_all | solution.py:34
  102.4 8.6 %all-to-all-done.1 = f32[16,1,2048]{2,1,0:T(1,128)S(1)} async-done(((f32[16,1,2048]{2,1,0:T(1,128)}), f32[16,1,2048]{2,1,0:T(1,128)S(1)}, u32[]{:S(2)}, u32[]{:S(2)}) %all-to-all-start.1) | async-done | bytes 131104 | tf_op jit(solution)/shard_map/all_to_all | solution.py:34
  113.2 22.9 %all-reduce.3 = (f32[64,64]{0,1:T(8,128)S(1)}, f32[64,64]{1,0:T(8,128)S(1)}, f32[64,64]{1,0:T(8,128)S(1)}) all-reduce(f32[64,64]{0,1:T(8,128)S(1)} %fusion.74, f32[64,64]{1,0:T(8,128)S(1)} %convolution_bitcast_fusion.6, f32[64,64]{1,0:T(8,128)S(1)} %fusion.54), channel_id=1, replica_groups=mesh['row_0'=8,'row_1'=4,'col_0'=8,'col_1'=2] {'row_0'}, use_global_device_ids=true, to_apply=%region_7.10 | all-reduce | flops 12288 | bytes 98304 | tf_op jit(solution)/shard_map/psum | solution.py:16
  136.1 14.2 %all-reduce.5 = (f32[64,64]{0,1:T(8,128)S(1)}, f32[64,64]{1,0:T(8,128)S(1)}, f32[64,64]{1,0:T(8,128)S(1)}) all-reduce(f32[64,64]{0,1:T(8,128)S(1)} %get-tuple-element.14, f32[64,64]{1,0:T(8,128)S(1)} %get-tuple-element.15, f32[64,64]{1,0:T(8,128)S(1)} %get-tuple-element.16), channel_id=1, replica_groups=mesh['row_0'=8,'row_1'=4,'col_0'=8,'col_1'=2] {'row_1'}, use_global_device_ids=true, to_apply=%region_8.11 | all-reduce | flops 12288 | bytes 98304 | tf_op jit(solution)/shard_map/psum | solution.py:16
  150.3 21.7 %all-reduce.1 = (f32[64,64]{0,1:T(8,128)S(1)}, f32[64,64]{1,0:T(8,128)S(1)}, f32[64,64]{1,0:T(8,128)S(1)}) all-reduce(f32[64,64]{0,1:T(8,128)S(1)} %get-tuple-element.20, f32[64,64]{1,0:T(8,128)S(1)} %get-tuple-element.21, f32[64,64]{1,0:T(8,128)S(1)} %get-tuple-element.22), channel_id=1, replica_groups=mesh['row_0'=8,'row_1'=4,'col_0'=8,'col_1'=2] {'col_0'}, use_global_device_ids=true, to_apply=%region_9.12 | all-reduce | flops 12288 | bytes 98304 | tf_op jit(solution)/shard_map/psum | solution.py:16
  172.0 21.3 %all-reduce.7 = (f32[64,64]{0,1:T(8,128)S(1)}, f32[64,64]{1,0:T(8,128)S(1)}, f32[64,64]{1,0:T(8,128)S(1)}) all-reduce(f32[64,64]{0,1:T(8,128)S(1)} %get-tuple-element.8, f32[64,64]{1,0:T(8,128)S(1)} %get-tuple-element.9, f32[64,64]{1,0:T(8,128)S(1)} %get-tuple-element.10), channel_id=1, replica_groups=mesh['row_0'=8,'row_1'=4,'col_0'=8,'col_1'=2] {'col_1'}, use_global_device_ids=true, to_apply=%region_10.13 | all-reduce | flops 12288 | bytes 98304 | tf_op jit(solution)/shard_map/psum | solution.py:16
  193.5 5.8 cholesky.89
  200.7 4.9 custom-call.11
  207.1 5.8 cholesky.100
  214.3 4.9 custom-call.12
  219.9 12.5 %all_to_all.31 = bf16[16,2,1024]{2,1,0:T(2,128)(2,1)S(1)} all-to-all(bf16[16,2,1024]{2,1,0:T(2,128)(2,1)S(1)} %reshape.250), channel_id=1, replica_groups=mesh['row_0'=8,'row_1'=4,'col_0'=8,'col_1'=2] {'col_0','col_1'}, dimensions={0} | all-to-all | bytes 131072 | tf_op jit(solution)/shard_map/all_to_all | solution.py:87
  232.7 10.1 %all_gather.20 = bf16[64,4,512]{2,0,1:T(8,128)(2,1)} all-gather(bf16[64,1,512]{2,0,1:T(8,128)(2,1)S(1)} %copy.97), channel_id=1, replica_groups=mesh['row_0'=8,'row_1'=4,'col_0'=8,'col_1'=2] {'row_1'}, dimensions={1}, use_global_device_ids=true | all-gather | bytes 327680 | tf_op jit(solution)/shard_map/all_gather | solution.py:22
  243.0 5.9 cholesky.122
  248.9 28.9 %all-gather.6.cloned.1.call-done = bf16[64,32,512]{2,0,1:T(8,128)(2,1)} async-done(((bf16[64,4,512]{2,0,1:T(8,128)(2,1)}), bf16[64,32,512]{2,0,1:T(8,128)(2,1)}) %all-gather.6.cloned.1.call-update) | async-done | bytes 2097168 | tf_op jit(solution)/shard_map/all_gather | solution.py:22
  277.8 2.8 copy.98
  280.5 2.6 reshape.207
  283.1 2.9 copy.99
  291.4 12.2 %all-to-all-start.3 = ((f32[16,1,2048]{2,1,0:T(1,128)}), f32[16,1,2048]{2,1,0:T(1,128)S(1)}, u32[]{:S(2)}, u32[]{:S(2)}) async-start(f32[16,1,2048]{2,1,0:T(1,128)} %reshape.252), calls=%async_computation.3 | async-start | bytes 262144 | tf_op jit(solution)/shard_map/all_to_all | solution.py:34
  305.1 4.9 custom-call.14
  310.0 2.4 all-to-all-done.3
  314.3 22.9 %all-reduce.2 = (f32[64,64]{1,0:T(8,128)S(1)}, f32[64,64]{1,0:T(8,128)S(1)}, f32[64,64]{1,0:T(8,128)S(1)}) all-reduce(f32[64,64]{1,0:T(8,128)S(1)} %fusion.78, f32[64,64]{1,0:T(8,128)S(1)} %fusion.81, f32[64,64]{1,0:T(8,128)S(1)} %fusion.79), channel_id=1, replica_groups=mesh['row_0'=8,'row_1'=4,'col_0'=8,'col_1'=2] {'row_0'}, use_global_device_ids=true, to_apply=%region_16.20 | all-reduce | flops 12288 | bytes 98304 | tf_op jit(solution)/shard_map/psum | solution.py:16
  337.2 14.2 %all-reduce.4 = (f32[64,64]{1,0:T(8,128)S(1)}, f32[64,64]{1,0:T(8,128)S(1)}, f32[64,64]{1,0:T(8,128)S(1)}) all-reduce(f32[64,64]{1,0:T(8,128)S(1)} %get-tuple-element.11, f32[64,64]{1,0:T(8,128)S(1)} %get-tuple-element.12, f32[64,64]{1,0:T(8,128)S(1)} %get-tuple-element.13), channel_id=1, replica_groups=mesh['row_0'=8,'row_1'=4,'col_0'=8,'col_1'=2] {'row_1'}, use_global_device_ids=true, to_apply=%region_17.21 | all-reduce | flops 12288 | bytes 98304 | tf_op jit(solution)/shard_map/psum | solution.py:16
  351.4 21.6 %all-reduce = (f32[64,64]{1,0:T(8,128)S(1)}, f32[64,64]{1,0:T(8,128)S(1)}, f32[64,64]{1,0:T(8,128)S(1)}) all-reduce(f32[64,64]{1,0:T(8,128)S(1)} %get-tuple-element.17, f32[64,64]{1,0:T(8,128)S(1)} %get-tuple-element.18, f32[64,64]{1,0:T(8,128)S(1)} %get-tuple-element.19), channel_id=1, replica_groups=mesh['row_0'=8,'row_1'=4,'col_0'=8,'col_1'=2] {'col_0'}, use_global_device_ids=true, to_apply=%region_18.22 | all-reduce | flops 12288 | bytes 98304 | tf_op jit(solution)/shard_map/psum | solution.py:16
  373.0 21.5 %all-reduce.6 = (f32[64,64]{1,0:T(8,128)S(1)}, f32[64,64]{1,0:T(8,128)S(1)}, f32[64,64]{1,0:T(8,128)S(1)}) all-reduce(f32[64,64]{1,0:T(8,128)S(1)} %get-tuple-element.4, f32[64,64]{1,0:T(8,128)S(1)} %get-tuple-element.6, f32[64,64]{1,0:T(8,128)S(1)} %get-tuple-element.7), channel_id=1, replica_groups=mesh['row_0'=8,'row_1'=4,'col_0'=8,'col_1'=2] {'col_1'}, use_global_device_ids=true, to_apply=%region_19.23 | all-reduce | flops 12288 | bytes 98304 | tf_op jit(solution)/shard_map/psum | solution.py:16
  394.7 5.8 cholesky.111
  401.9 4.9 custom-call.13
  408.9 12.3 %all_to_all.32 = bf16[16,2,1024]{2,1,0:T(2,128)(2,1)S(1)} all-to-all(bf16[16,2,1024]{2,1,0:T(2,128)(2,1)S(1)} %reshape.254), channel_id=1, replica_groups=mesh['row_0'=8,'row_1'=4,'col_0'=8,'col_1'=2] {'col_0','col_1'}, dimensions={0} | all-to-all | bytes 131072 | tf_op jit(solution)/shard_map/all_to_all | solution.py:87
  421.5 10.1 %all_gather.22 = bf16[64,4,512]{2,0,1:T(8,128)(2,1)} all-gather(bf16[64,1,512]{2,0,1:T(8,128)(2,1)S(1)} %copy.108), channel_id=1, replica_groups=mesh['row_0'=8,'row_1'=4,'col_0'=8,'col_1'=2] {'row_1'}, dimensions={1}, use_global_device_ids=true | all-gather | bytes 327680 | tf_op jit(solution)/shard_map/all_gather | solution.py:22
  431.6 34.9 %all-gather.8.cloned.1.call-done = bf16[64,32,512]{2,0,1:T(8,128)(2,1)} async-done(((bf16[64,4,512]{2,0,1:T(8,128)(2,1)}), bf16[64,32,512]{2,0,1:T(8,128)(2,1)}) %all-gather.8.cloned.1.call-update) | async-done | bytes 2097168 | tf_op jit(solution)/shard_map/all_gather | solution.py:22
  466.5 2.8 copy.109
  469.3 2.6 reshape.210
  471.9 2.9 copy.110
  476.2 1.9 convolution_bitcast_fusion
  480.1 12.2 %all-to-all-start.5 = ((f32[16,1,2048]{2,1,0:T(1,128)}), f32[16,1,2048]{2,1,0:T(1,128)S(1)}, u32[]{:S(2)}, u32[]{:S(2)}) async-start(f32[16,1,2048]{2,1,0:T(1,128)} %reshape.256), calls=%async_computation.5 | async-start | bytes 262144 | tf_op jit(solution)/shard_map/all_to_all | solution.py:34
  492.6 8.6 %all-to-all-done.5 = f32[16,1,2048]{2,1,0:T(1,128)S(1)} async-done(((f32[16,1,2048]{2,1,0:T(1,128)}), f32[16,1,2048]{2,1,0:T(1,128)S(1)}, u32[]{:S(2)}, u32[]{:S(2)}) %all-to-all-start.5) | async-done | bytes 131104 | tf_op jit(solution)/shard_map/all_to_all | solution.py:34
  502.6 22.1 %psum.232 = f32[64,64]{1,0:T(8,128)S(1)} all-reduce(f32[64,64]{1,0:T(8,128)S(1)} %fusion.53), channel_id=1, replica_groups=mesh['row_0'=8,'row_1'=4,'col_0'=8,'col_1'=2] {'row_0'}, use_global_device_ids=true, to_apply=%region_29.33 | all-reduce | flops 4096 | bytes 32768 | tf_op jit(solution)/shard_map/psum | solution.py:16
  524.6 13.2 %psum.233 = f32[64,64]{1,0:T(8,128)S(1)} all-reduce(f32[64,64]{1,0:T(8,128)S(1)} %psum.232), channel_id=1, replica_groups=mesh['row_0'=8,'row_1'=4,'col_0'=8,'col_1'=2] {'row_1'}, use_global_device_ids=true, to_apply=%region_30.34 | all-reduce | flops 4096 | bytes 32768 | tf_op jit(solution)/shard_map/psum | solution.py:16
  537.9 20.4 %psum.234 = f32[64,64]{1,0:T(8,128)S(1)} all-reduce(f32[64,64]{1,0:T(8,128)S(1)} %psum.233), channel_id=1, replica_groups=mesh['row_0'=8,'row_1'=4,'col_0'=8,'col_1'=2] {'col_0'}, use_global_device_ids=true, to_apply=%region_31.35 | all-reduce | flops 4096 | bytes 32768 | tf_op jit(solution)/shard_map/psum | solution.py:16
  558.2 21.0 %psum.235 = f32[64,64]{1,0:T(8,128)S(1)} all-reduce(f32[64,64]{1,0:T(8,128)S(1)} %psum.234), channel_id=1, replica_groups=mesh['row_0'=8,'row_1'=4,'col_0'=8,'col_1'=2] {'col_1'}, use_global_device_ids=true, to_apply=%region_32.36 | all-reduce | flops 4096 | bytes 32768 | tf_op jit(solution)/shard_map/psum | solution.py:16
  579.4 5.8 cholesky.133
  586.6 4.9 custom-call.15
  (122 shorter events, 34.7 us)
Async XLA Ops:
  7.2 78.8 %copy-start = (bf16[1,32,1,128,128]{4,3,2,1,0:T(8,128)(2,1)S(1)}, bf16[1,32,1,128,128]{4,3,2,1,0:T(8,128)(2,1)}, u32[]{:S(2)}) copy-start(bf16[1,32,1,128,128]{4,3,2,1,0:T(8,128)(2,1)} %param.13) | copy-start | bytes 3145732
  7.2 69.1 %all-gather.4.cloned.1.call-start = ((), (), s32[]{:S(2)}) async-start(), calls=%async_computation.6 | async-start | bytes 2359296 | tf_op jit(solution)/shard_map/all_gather | solution.py:22
  84.6 3.3 copy-start.3
  86.0 16.2 %copy-start.1 = (f32[64,32]{0,1:T(8,128)S(1)}, f32[64,32]{0,1:T(8,128)}, u32[]{:S(2)}) copy-start(f32[64,32]{0,1:T(8,128)} %param.11) | copy-start | bytes 24580
  87.9 24.7 %copy-start.2 = (f32[32]{0:T(128)S(1)}, f32[32]{0:T(128)}, u32[]{:S(2)}) copy-start(f32[32]{0:T(128)} %param.12) | copy-start | bytes 388
  89.9 21.1 %all-to-all-start.1 = ((f32[16,1,2048]{2,1,0:T(1,128)}), f32[16,1,2048]{2,1,0:T(1,128)S(1)}, u32[]{:S(2)}, u32[]{:S(2)}) async-start(f32[16,1,2048]{2,1,0:T(1,128)} %reshape.248), calls=%async_computation.1 | async-start | bytes 262144 | tf_op jit(solution)/shard_map/all_to_all | solution.py:34
  102.1 175.6 %all-gather.6.cloned.1.call-start = ((), (), s32[]{:S(2)}) async-start(), calls=%async_computation.7 | async-start | bytes 2359296 | tf_op jit(solution)/shard_map/all_gather | solution.py:22
  291.4 21.1 %all-to-all-start.3 = ((f32[16,1,2048]{2,1,0:T(1,128)}), f32[16,1,2048]{2,1,0:T(1,128)S(1)}, u32[]{:S(2)}, u32[]{:S(2)}) async-start(f32[16,1,2048]{2,1,0:T(1,128)} %reshape.252), calls=%async_computation.3 | async-start | bytes 262144 | tf_op jit(solution)/shard_map/all_to_all | solution.py:34
  303.5 163.0 %all-gather.8.cloned.1.call-start = ((), (), s32[]{:S(2)}) async-start(), calls=%async_computation.8 | async-start | bytes 2359296 | tf_op jit(solution)/shard_map/all_gather | solution.py:22
  480.1 21.1 %all-to-all-start.5 = ((f32[16,1,2048]{2,1,0:T(1,128)}), f32[16,1,2048]{2,1,0:T(1,128)S(1)}, u32[]{:S(2)}, u32[]{:S(2)}) async-start(f32[16,1,2048]{2,1,0:T(1,128)} %reshape.256), calls=%async_computation.5 | async-start | bytes 262144 | tf_op jit(solution)/shard_map/all_to_all | solution.py:34
Sparse Core Ops, SparseCore 0:
  38.4 37.8 all-gather.3
  243.0 34.7 all-gather.5
  431.7 34.7 all-gather.7
